TPU v7x, 128 devices: a whole 4x4x4 slice. The times are simulated.
128 devices in a mesh: tiles: 16 (over y, z), lag: 8 (over x, core).
Axes of the slice: x: 4, y: 4, z: 4, core: 2. Of those that a mesh axis runs over, the one named last changes fastest.
Arguments:
- spectra: bfloat16 [32, 2, 2, 128, 8192], P('tiles', None, None, None, 'lag'), may hold values from -6 to 6
- requests: int32 [16, 6], replicated, may hold values from 0 to 31, as said below
- pairs: int32 [16, 3, 2], P('tiles'), may hold values from 0 to 5, as said below
- counts: int32 [16], P('tiles'), may hold values from 2 to 3, as said below
Outputs:
- stacked_lags: float32 [48, 64, 128, 128], P('tiles', 'lag')
Inputs may be any that keep to these rules, and one draw needn't show every extreme that they name: Block b is held by index b // 2 of tiles; each row of requests names 6 blocks held by 6 different indices. Each row's 3 entries are pairs (i, j) of request slots with i < j that together use every request slot once. The first counts[d] slots of row d are live, the others give zeros; some index has 3.
All inputs are finite; a program needn't handle non-finite values.
Results may differ from a plain program's by a relative error of at most 0.012.
Values may be sent and summed in bfloat16 or wider, within the bound.
A program may use at most 128 MiB of HBM per device.

v0:
```python
import math
import jax
import jax.numpy as jnp
from jax import lax
from jax.sharding import PartitionSpec as P

F = 8192
W = 2
LAGS = 64
FBLK = 128


def phase_table(freq_first, width):
    frequencies = freq_first + jnp.arange(width, dtype=jnp.int32)
    shifts = (jnp.arange(LAGS, dtype=jnp.int32) - LAGS // 2) % F
    phase_index = frequencies[:, None] * shifts[None, :] % F
    angles = phase_index.astype(jnp.float32) * (2.0 * math.pi / F)
    return jnp.concatenate([jnp.cos(angles), -jnp.sin(angles)], axis=0).astype(jnp.bfloat16)


def cross_block(left_part, right_part):
    left_wide = left_part.astype(jnp.float32)
    right_wide = right_part.astype(jnp.float32)
    real_part = jnp.sum(
        left_wide[:, 0, :, None, :] * right_wide[:, 0, None, :, :]
        + left_wide[:, 1, :, None, :] * right_wide[:, 1, None, :, :],
        axis=0,
    )
    imag_part = jnp.sum(
        left_wide[:, 1, :, None, :] * right_wide[:, 0, None, :, :]
        - left_wide[:, 0, :, None, :] * right_wide[:, 1, None, :, :],
        axis=0,
    )
    channels = left_part.shape[2]
    return (
        jnp.concatenate([real_part, imag_part], axis=-1)
        .reshape(channels * channels, -1)
        .astype(jnp.bfloat16)
    )


def band_sum(left_block, right_block, band_first):
    channels = left_block.shape[2]
    block_count = left_block.shape[-1] // FBLK

    def block_step(running, block_index):
        offset = block_index * FBLK
        left_part = lax.dynamic_slice_in_dim(left_block, offset, FBLK, 3)
        right_part = lax.dynamic_slice_in_dim(right_block, offset, FBLK, 3)
        stacked = cross_block(left_part, right_part)
        phases = phase_table(band_first + offset, FBLK)
        return (
            running
            + lax.dot_general(
                phases, stacked, (((0,), (1,)), ((), ())), preferred_element_type=jnp.float32
            ),
            None,
        )

    running = jnp.zeros((LAGS, channels * channels), jnp.float32)
    running, unused = lax.scan(block_step, running, jnp.arange(block_count, dtype=jnp.int32))
    return running


def per_device(spectra, requests, pairs, counts):
    channels = spectra.shape[3]
    own_index = lax.axis_index("tiles")
    wanted = lax.dynamic_index_in_dim(requests, own_index, 0, keepdims=False)
    empty = jnp.zeros((wanted.shape[0],) + spectra.shape[1:], jnp.bfloat16)
    shards = lax.all_gather(spectra, "tiles", axis=0, tiled=True)
    inside = (wanted >= 0) & (wanted < shards.shape[0])
    taken = jnp.take(shards, jnp.clip(wanted, 0, shards.shape[0] - 1), axis=0)
    needed = jnp.where(inside[:, None, None, None, None], taken, empty)
    band_first = lax.axis_index("lag") * spectra.shape[-1]
    norm_factor = 1.0 / math.sqrt(2.0 * W * F)
    live_count = counts[0]
    tile_pairs = pairs[0]
    slot_total = tile_pairs.shape[0]
    terms = []
    for slot_index in range(slot_total):
        left_block = jnp.take(needed, tile_pairs[slot_index, 0], axis=0)
        right_block = jnp.take(needed, tile_pairs[slot_index, 1], axis=0)
        result = band_sum(left_block, right_block, band_first) * norm_factor
        terms.append(jnp.where(slot_index < live_count, result, jnp.zeros_like(result)))
    partial_terms = jnp.stack(terms).reshape(slot_total, LAGS, channels, channels)
    return lax.psum_scatter(
        partial_terms.astype(jnp.bfloat16), "lag", scatter_dimension=1, tiled=True
    ).astype(jnp.float32)


def solution(mesh):
    placed = (P("tiles", None, None, None, "lag"), P(), P("tiles", None, None), P("tiles"))
    return jax.shard_map(
        per_device,
        mesh=mesh,
        in_specs=placed,
        out_specs=P("tiles", "lag", None, None),
        check_vma=False,
    )
```

profile of v0, /device:TPU:1, one launch (start us, length us, event | category | flops | bytes accessed | tf_op | source)
XLA Modules:
  0.0 1019.2 jit_solution(7977212312652234884)
XLA Ops:
  22.7 187.3 %all-gather.2.cloned.1.call-done = bf16[32,2,2,128,1024]{4,3,2,1,0:T(8,128)(2,1)} async-done(((bf16[2,2,2,128,1024]{4,3,2,1,0:T(8,128)(2,1)}), bf16[32,2,2,128,1024]{4,3,2,1,0:T(8,128)(2,1)}) %all-gather.2.cloned.1.call-update) | async-done | bytes 33554448 | tf_op jit(solution)/shard_map/all_gather | solution.py:70
  221.3 236.1 %while.40 = (s32[]{:T(128)}, f32[64,16384]{1,0:T(8,128)}, s32[8]{0:T(128)S(1)}, s32[]{:T(128)}, bf16[2,2,128,1024]{3,2,1,0:T(8,128)(2,1)S(1)}, /*index=5*/bf16[2...) while((s32[]{:T(128)}, f32[64,16384]{1,0:T(8,128)}, ...), condition=%wide.region_3.5_spmd.clone, body=%wide.region_0.0_spmd.clone.sunk | while | flops 585442176 | bytes 44893884 | solution.py:61
  222.8 11.7 %add_reduce_fusion.6 = (bf16[128,128,128]{2,1,0:T(8,128)(2,1)S(1)}, bf16[128,128,128]{2,1,0:T(8,128)(2,1)}) fusion(f32[2,128,128]{2,1,0:T(8,128)S(1)} %get-tuple-element.564, f32[2,128,128]{2,1,0:T(8,128)S(1)} %get-tuple-element.566, f32[2,128,128]{2,1,0:T(8,128)S(1)} %get-tuple-element.567, f32[2,128,128]{2,1,0:T(8,128)S(1)} %get-tuple-element.568), kind=kLoop, calls=%fused_computation.3.clone.1 | loop fusion | flops 29360128 | bytes 8912896 | tf_op jit(solution)/shard_map/while/body/eval_jaxpr/reduce_sum | solution.py:24
  251.3 11.7 %add_reduce_fusion.6 = (bf16[128,128,128]{2,1,0:T(8,128)(2,1)S(1)}, bf16[128,128,128]{2,1,0:T(8,128)(2,1)}) fusion(f32[2,128,128]{2,1,0:T(8,128)S(1)} %get-tuple-element.564, f32[2,128,128]{2,1,0:T(8,128)S(1)} %get-tuple-element.566, f32[2,128,128]{2,1,0:T(8,128)S(1)} %get-tuple-element.567, f32[2,128,128]{2,1,0:T(8,128)S(1)} %get-tuple-element.568), kind=kLoop, calls=%fused_computation.3.clone.1 | loop fusion | flops 29360128 | bytes 8912896 | tf_op jit(solution)/shard_map/while/body/eval_jaxpr/reduce_sum | solution.py:24
  280.9 11.7 %add_reduce_fusion.6 = (bf16[128,128,128]{2,1,0:T(8,128)(2,1)S(1)}, bf16[128,128,128]{2,1,0:T(8,128)(2,1)}) fusion(f32[2,128,128]{2,1,0:T(8,128)S(1)} %get-tuple-element.564, f32[2,128,128]{2,1,0:T(8,128)S(1)} %get-tuple-element.566, f32[2,128,128]{2,1,0:T(8,128)S(1)} %get-tuple-element.567, f32[2,128,128]{2,1,0:T(8,128)S(1)} %get-tuple-element.568), kind=kLoop, calls=%fused_computation.3.clone.1 | loop fusion | flops 29360128 | bytes 8912896 | tf_op jit(solution)/shard_map/while/body/eval_jaxpr/reduce_sum | solution.py:24
  310.6 11.7 %add_reduce_fusion.6 = (bf16[128,128,128]{2,1,0:T(8,128)(2,1)S(1)}, bf16[128,128,128]{2,1,0:T(8,128)(2,1)}) fusion(f32[2,128,128]{2,1,0:T(8,128)S(1)} %get-tuple-element.564, f32[2,128,128]{2,1,0:T(8,128)S(1)} %get-tuple-element.566, f32[2,128,128]{2,1,0:T(8,128)S(1)} %get-tuple-element.567, f32[2,128,128]{2,1,0:T(8,128)S(1)} %get-tuple-element.568), kind=kLoop, calls=%fused_computation.3.clone.1 | loop fusion | flops 29360128 | bytes 8912896 | tf_op jit(solution)/shard_map/while/body/eval_jaxpr/reduce_sum | solution.py:24
  340.2 11.7 %add_reduce_fusion.6 = (bf16[128,128,128]{2,1,0:T(8,128)(2,1)S(1)}, bf16[128,128,128]{2,1,0:T(8,128)(2,1)}) fusion(f32[2,128,128]{2,1,0:T(8,128)S(1)} %get-tuple-element.564, f32[2,128,128]{2,1,0:T(8,128)S(1)} %get-tuple-element.566, f32[2,128,128]{2,1,0:T(8,128)S(1)} %get-tuple-element.567, f32[2,128,128]{2,1,0:T(8,128)S(1)} %get-tuple-element.568), kind=kLoop, calls=%fused_computation.3.clone.1 | loop fusion | flops 29360128 | bytes 8912896 | tf_op jit(solution)/shard_map/while/body/eval_jaxpr/reduce_sum | solution.py:24
  369.9 11.7 %add_reduce_fusion.6 = (bf16[128,128,128]{2,1,0:T(8,128)(2,1)S(1)}, bf16[128,128,128]{2,1,0:T(8,128)(2,1)}) fusion(f32[2,128,128]{2,1,0:T(8,128)S(1)} %get-tuple-element.564, f32[2,128,128]{2,1,0:T(8,128)S(1)} %get-tuple-element.566, f32[2,128,128]{2,1,0:T(8,128)S(1)} %get-tuple-element.567, f32[2,128,128]{2,1,0:T(8,128)S(1)} %get-tuple-element.568), kind=kLoop, calls=%fused_computation.3.clone.1 | loop fusion | flops 29360128 | bytes 8912896 | tf_op jit(solution)/shard_map/while/body/eval_jaxpr/reduce_sum | solution.py:24
  399.5 11.7 %add_reduce_fusion.6 = (bf16[128,128,128]{2,1,0:T(8,128)(2,1)S(1)}, bf16[128,128,128]{2,1,0:T(8,128)(2,1)}) fusion(f32[2,128,128]{2,1,0:T(8,128)S(1)} %get-tuple-element.564, f32[2,128,128]{2,1,0:T(8,128)S(1)} %get-tuple-element.566, f32[2,128,128]{2,1,0:T(8,128)S(1)} %get-tuple-element.567, f32[2,128,128]{2,1,0:T(8,128)S(1)} %get-tuple-element.568), kind=kLoop, calls=%fused_computation.3.clone.1 | loop fusion | flops 29360128 | bytes 8912896 | tf_op jit(solution)/shard_map/while/body/eval_jaxpr/reduce_sum | solution.py:24
  429.2 11.7 %add_reduce_fusion.6 = (bf16[128,128,128]{2,1,0:T(8,128)(2,1)S(1)}, bf16[128,128,128]{2,1,0:T(8,128)(2,1)}) fusion(f32[2,128,128]{2,1,0:T(8,128)S(1)} %get-tuple-element.564, f32[2,128,128]{2,1,0:T(8,128)S(1)} %get-tuple-element.566, f32[2,128,128]{2,1,0:T(8,128)S(1)} %get-tuple-element.567, f32[2,128,128]{2,1,0:T(8,128)S(1)} %get-tuple-element.568), kind=kLoop, calls=%fused_computation.3.clone.1 | loop fusion | flops 29360128 | bytes 8912896 | tf_op jit(solution)/shard_map/while/body/eval_jaxpr/reduce_sum | solution.py:24
  460.7 244.2 %while.41 = (s32[]{:T(128)}, f32[64,16384]{1,0:T(8,128)}, s32[8]{0:T(128)S(1)}, s32[]{:T(128)}, bf16[2,2,128,1024]{3,2,1,0:T(8,128)(2,1)}, /*index=5*/bf16[2,2,1...) while((s32[]{:T(128)}, f32[64,16384]{1,0:T(8,128)}, s32[8]{0:T(128)S(1)}, ...), condition=%wide.region_7.9_spmd.clone, body=%wide.region_4.8_spmd.clone.sunk | while | flops 585442176 | bytes 44893884 | solution.py:61
  463.2 11.7 %add_reduce_fusion.7 = (bf16[128,128,128]{2,1,0:T(8,128)(2,1)S(1)}, bf16[128,128,128]{2,1,0:T(8,128)(2,1)}) fusion(f32[2,128,128]{2,1,0:T(8,128)S(1)} %get-tuple-element.580, f32[2,128,128]{2,1,0:T(8,128)S(1)} %get-tuple-element.582, f32[2,128,128]{2,1,0:T(8,128)S(1)} %get-tuple-element.583, f32[2,128,128]{2,1,0:T(8,128)S(1)} %get-tuple-element.584), kind=kLoop, calls=%fused_computation.34.clone.1 | loop fusion | flops 29360128 | bytes 8912896 | tf_op jit(solution)/shard_map/while/body/eval_jaxpr/reduce_sum | solution.py:24
  492.7 11.7 %add_reduce_fusion.7 = (bf16[128,128,128]{2,1,0:T(8,128)(2,1)S(1)}, bf16[128,128,128]{2,1,0:T(8,128)(2,1)}) fusion(f32[2,128,128]{2,1,0:T(8,128)S(1)} %get-tuple-element.580, f32[2,128,128]{2,1,0:T(8,128)S(1)} %get-tuple-element.582, f32[2,128,128]{2,1,0:T(8,128)S(1)} %get-tuple-element.583, f32[2,128,128]{2,1,0:T(8,128)S(1)} %get-tuple-element.584), kind=kLoop, calls=%fused_computation.34.clone.1 | loop fusion | flops 29360128 | bytes 8912896 | tf_op jit(solution)/shard_map/while/body/eval_jaxpr/reduce_sum | solution.py:24
  511.7 9.3 convolution_add_fusion.7
  523.3 11.7 %add_reduce_fusion.7 = (bf16[128,128,128]{2,1,0:T(8,128)(2,1)S(1)}, bf16[128,128,128]{2,1,0:T(8,128)(2,1)}) fusion(f32[2,128,128]{2,1,0:T(8,128)S(1)} %get-tuple-element.580, f32[2,128,128]{2,1,0:T(8,128)S(1)} %get-tuple-element.582, f32[2,128,128]{2,1,0:T(8,128)S(1)} %get-tuple-element.583, f32[2,128,128]{2,1,0:T(8,128)S(1)} %get-tuple-element.584), kind=kLoop, calls=%fused_computation.34.clone.1 | loop fusion | flops 29360128 | bytes 8912896 | tf_op jit(solution)/shard_map/while/body/eval_jaxpr/reduce_sum | solution.py:24
  554.0 11.7 %add_reduce_fusion.7 = (bf16[128,128,128]{2,1,0:T(8,128)(2,1)S(1)}, bf16[128,128,128]{2,1,0:T(8,128)(2,1)}) fusion(f32[2,128,128]{2,1,0:T(8,128)S(1)} %get-tuple-element.580, f32[2,128,128]{2,1,0:T(8,128)S(1)} %get-tuple-element.582, f32[2,128,128]{2,1,0:T(8,128)S(1)} %get-tuple-element.583, f32[2,128,128]{2,1,0:T(8,128)S(1)} %get-tuple-element.584), kind=kLoop, calls=%fused_computation.34.clone.1 | loop fusion | flops 29360128 | bytes 8912896 | tf_op jit(solution)/shard_map/while/body/eval_jaxpr/reduce_sum | solution.py:24
  573.0 9.3 convolution_add_fusion.7
  584.6 11.7 %add_reduce_fusion.7 = (bf16[128,128,128]{2,1,0:T(8,128)(2,1)S(1)}, bf16[128,128,128]{2,1,0:T(8,128)(2,1)}) fusion(f32[2,128,128]{2,1,0:T(8,128)S(1)} %get-tuple-element.580, f32[2,128,128]{2,1,0:T(8,128)S(1)} %get-tuple-element.582, f32[2,128,128]{2,1,0:T(8,128)S(1)} %get-tuple-element.583, f32[2,128,128]{2,1,0:T(8,128)S(1)} %get-tuple-element.584), kind=kLoop, calls=%fused_computation.34.clone.1 | loop fusion | flops 29360128 | bytes 8912896 | tf_op jit(solution)/shard_map/while/body/eval_jaxpr/reduce_sum | solution.py:24
  615.3 11.7 %add_reduce_fusion.7 = (bf16[128,128,128]{2,1,0:T(8,128)(2,1)S(1)}, bf16[128,128,128]{2,1,0:T(8,128)(2,1)}) fusion(f32[2,128,128]{2,1,0:T(8,128)S(1)} %get-tuple-element.580, f32[2,128,128]{2,1,0:T(8,128)S(1)} %get-tuple-element.582, f32[2,128,128]{2,1,0:T(8,128)S(1)} %get-tuple-element.583, f32[2,128,128]{2,1,0:T(8,128)S(1)} %get-tuple-element.584), kind=kLoop, calls=%fused_computation.34.clone.1 | loop fusion | flops 29360128 | bytes 8912896 | tf_op jit(solution)/shard_map/while/body/eval_jaxpr/reduce_sum | solution.py:24
  645.9 11.7 %add_reduce_fusion.7 = (bf16[128,128,128]{2,1,0:T(8,128)(2,1)S(1)}, bf16[128,128,128]{2,1,0:T(8,128)(2,1)}) fusion(f32[2,128,128]{2,1,0:T(8,128)S(1)} %get-tuple-element.580, f32[2,128,128]{2,1,0:T(8,128)S(1)} %get-tuple-element.582, f32[2,128,128]{2,1,0:T(8,128)S(1)} %get-tuple-element.583, f32[2,128,128]{2,1,0:T(8,128)S(1)} %get-tuple-element.584), kind=kLoop, calls=%fused_computation.34.clone.1 | loop fusion | flops 29360128 | bytes 8912896 | tf_op jit(solution)/shard_map/while/body/eval_jaxpr/reduce_sum | solution.py:24
  664.9 9.3 convolution_add_fusion.7
  676.6 11.7 %add_reduce_fusion.7 = (bf16[128,128,128]{2,1,0:T(8,128)(2,1)S(1)}, bf16[128,128,128]{2,1,0:T(8,128)(2,1)}) fusion(f32[2,128,128]{2,1,0:T(8,128)S(1)} %get-tuple-element.580, f32[2,128,128]{2,1,0:T(8,128)S(1)} %get-tuple-element.582, f32[2,128,128]{2,1,0:T(8,128)S(1)} %get-tuple-element.583, f32[2,128,128]{2,1,0:T(8,128)S(1)} %get-tuple-element.584), kind=kLoop, calls=%fused_computation.34.clone.1 | loop fusion | flops 29360128 | bytes 8912896 | tf_op jit(solution)/shard_map/while/body/eval_jaxpr/reduce_sum | solution.py:24
  709.5 243.4 %while.42 = (s32[]{:T(128)}, f32[64,16384]{1,0:T(8,128)}, s32[8]{0:T(128)S(1)}, s32[]{:T(128)}, bf16[2,2,128,1024]{3,2,1,0:T(8,128)(2,1)}, /*index=5*/bf16[2,2,1...) while((s32[]{:T(128)}, f32[64,16384]{1,0:T(8,128)}, s32[8]{0:T(128)S(1)}, ...), condition=%wide.region_11.13_spmd.clone, body=%wide.region_8.12_spmd.clone.sunk | while | flops 585442176 | bytes 44893884 | solution.py:61
  711.9 11.7 %add_reduce_fusion.8 = (bf16[128,128,128]{2,1,0:T(8,128)(2,1)S(1)}, bf16[128,128,128]{2,1,0:T(8,128)(2,1)}) fusion(f32[2,128,128]{2,1,0:T(8,128)S(1)} %get-tuple-element.596, f32[2,128,128]{2,1,0:T(8,128)S(1)} %get-tuple-element.598, f32[2,128,128]{2,1,0:T(8,128)S(1)} %get-tuple-element.599, f32[2,128,128]{2,1,0:T(8,128)S(1)} %get-tuple-element.600), kind=kLoop, calls=%fused_computation.65.clone.1 | loop fusion | flops 29360128 | bytes 8912896 | tf_op jit(solution)/shard_map/while/body/eval_jaxpr/reduce_sum | solution.py:24
  741.3 11.7 %add_reduce_fusion.8 = (bf16[128,128,128]{2,1,0:T(8,128)(2,1)S(1)}, bf16[128,128,128]{2,1,0:T(8,128)(2,1)}) fusion(f32[2,128,128]{2,1,0:T(8,128)S(1)} %get-tuple-element.596, f32[2,128,128]{2,1,0:T(8,128)S(1)} %get-tuple-element.598, f32[2,128,128]{2,1,0:T(8,128)S(1)} %get-tuple-element.599, f32[2,128,128]{2,1,0:T(8,128)S(1)} %get-tuple-element.600), kind=kLoop, calls=%fused_computation.65.clone.1 | loop fusion | flops 29360128 | bytes 8912896 | tf_op jit(solution)/shard_map/while/body/eval_jaxpr/reduce_sum | solution.py:24
  771.9 11.7 %add_reduce_fusion.8 = (bf16[128,128,128]{2,1,0:T(8,128)(2,1)S(1)}, bf16[128,128,128]{2,1,0:T(8,128)(2,1)}) fusion(f32[2,128,128]{2,1,0:T(8,128)S(1)} %get-tuple-element.596, f32[2,128,128]{2,1,0:T(8,128)S(1)} %get-tuple-element.598, f32[2,128,128]{2,1,0:T(8,128)S(1)} %get-tuple-element.599, f32[2,128,128]{2,1,0:T(8,128)S(1)} %get-tuple-element.600), kind=kLoop, calls=%fused_computation.65.clone.1 | loop fusion | flops 29360128 | bytes 8912896 | tf_op jit(solution)/shard_map/while/body/eval_jaxpr/reduce_sum | solution.py:24
  802.4 11.7 %add_reduce_fusion.8 = (bf16[128,128,128]{2,1,0:T(8,128)(2,1)S(1)}, bf16[128,128,128]{2,1,0:T(8,128)(2,1)}) fusion(f32[2,128,128]{2,1,0:T(8,128)S(1)} %get-tuple-element.596, f32[2,128,128]{2,1,0:T(8,128)S(1)} %get-tuple-element.598, f32[2,128,128]{2,1,0:T(8,128)S(1)} %get-tuple-element.599, f32[2,128,128]{2,1,0:T(8,128)S(1)} %get-tuple-element.600), kind=kLoop, calls=%fused_computation.65.clone.1 | loop fusion | flops 29360128 | bytes 8912896 | tf_op jit(solution)/shard_map/while/body/eval_jaxpr/reduce_sum | solution.py:24
  833.0 11.7 %add_reduce_fusion.8 = (bf16[128,128,128]{2,1,0:T(8,128)(2,1)S(1)}, bf16[128,128,128]{2,1,0:T(8,128)(2,1)}) fusion(f32[2,128,128]{2,1,0:T(8,128)S(1)} %get-tuple-element.596, f32[2,128,128]{2,1,0:T(8,128)S(1)} %get-tuple-element.598, f32[2,128,128]{2,1,0:T(8,128)S(1)} %get-tuple-element.599, f32[2,128,128]{2,1,0:T(8,128)S(1)} %get-tuple-element.600), kind=kLoop, calls=%fused_computation.65.clone.1 | loop fusion | flops 29360128 | bytes 8912896 | tf_op jit(solution)/shard_map/while/body/eval_jaxpr/reduce_sum | solution.py:24
  863.6 11.7 %add_reduce_fusion.8 = (bf16[128,128,128]{2,1,0:T(8,128)(2,1)S(1)}, bf16[128,128,128]{2,1,0:T(8,128)(2,1)}) fusion(f32[2,128,128]{2,1,0:T(8,128)S(1)} %get-tuple-element.596, f32[2,128,128]{2,1,0:T(8,128)S(1)} %get-tuple-element.598, f32[2,128,128]{2,1,0:T(8,128)S(1)} %get-tuple-element.599, f32[2,128,128]{2,1,0:T(8,128)S(1)} %get-tuple-element.600), kind=kLoop, calls=%fused_computation.65.clone.1 | loop fusion | flops 29360128 | bytes 8912896 | tf_op jit(solution)/shard_map/while/body/eval_jaxpr/reduce_sum | solution.py:24
  894.1 11.7 %add_reduce_fusion.8 = (bf16[128,128,128]{2,1,0:T(8,128)(2,1)S(1)}, bf16[128,128,128]{2,1,0:T(8,128)(2,1)}) fusion(f32[2,128,128]{2,1,0:T(8,128)S(1)} %get-tuple-element.596, f32[2,128,128]{2,1,0:T(8,128)S(1)} %get-tuple-element.598, f32[2,128,128]{2,1,0:T(8,128)S(1)} %get-tuple-element.599, f32[2,128,128]{2,1,0:T(8,128)S(1)} %get-tuple-element.600), kind=kLoop, calls=%fused_computation.65.clone.1 | loop fusion | flops 29360128 | bytes 8912896 | tf_op jit(solution)/shard_map/while/body/eval_jaxpr/reduce_sum | solution.py:24
  924.7 11.7 %add_reduce_fusion.8 = (bf16[128,128,128]{2,1,0:T(8,128)(2,1)S(1)}, bf16[128,128,128]{2,1,0:T(8,128)(2,1)}) fusion(f32[2,128,128]{2,1,0:T(8,128)S(1)} %get-tuple-element.596, f32[2,128,128]{2,1,0:T(8,128)S(1)} %get-tuple-element.598, f32[2,128,128]{2,1,0:T(8,128)S(1)} %get-tuple-element.599, f32[2,128,128]{2,1,0:T(8,128)S(1)} %get-tuple-element.600), kind=kLoop, calls=%fused_computation.65.clone.1 | loop fusion | flops 29360128 | bytes 8912896 | tf_op jit(solution)/shard_map/while/body/eval_jaxpr/reduce_sum | solution.py:24
  967.2 42.6 %reduce-scatter.5.cloned.1.call-done = bf16[8,49152]{1,0:T(8,128)(2,1)} async-done(((bf16[64,49152]{1,0:T(8,128)(2,1)}), bf16[8,49152]{1,0:T(8,128)(2,1)}) %reduce-scatter.5.cloned.1.call-update) | async-done | bytes 786448
  (293 shorter events, 439.3 us)
Async XLA Ops:
  6.5 203.4 %all-gather.2.cloned.1.call-start = ((), (), s32[]{:S(2)}) async-start(), calls=%async_computation.1 | async-start | bytes 35651584 | tf_op jit(solution)/shard_map/all_gather | solution.py:70
  7.3 1002.5 %reduce-scatter.5.cloned.1.call-start = ((), (), s32[]{:S(2)}) async-start(), calls=%async_computation.2 | async-start | bytes 7077888
  952.9 3.5 copy-start
Sparse Core Ops, SparseCore 0:
  9.5 200.4 all-gather.1
  967.3 42.4 reduce-scatter.4
where the time goes:
time: 1020 us
  other arithmetic  475 us (47%)
  waiting for transfers between devices  231 us (23%)
  matrix products  218 us (21%)
  local copies, waits for them, and re-layouts  53.4 us (5%)
  between operations  25.5 us (2%)
  loops' own time  16.6 us (2%)
    reduce_sum x24, other arithmetic, cross_block(): jnp.sum(left_wide[:, 0, :, None, :] * right_wide[:, 0, None, :, :] + left...  280 us
    dot_general x24, matrix products, block_step(): lax.dot_general(phases, stacked, (((0,), (1,)), ((), ())), preferred_elem...  218 us
    all_gather x1, waiting for transfers between devices, per_device(): shards = lax.all_gather(spectra, 'tiles', axis=0, tiled=True)  187 us
    concatenate x24, other arithmetic, cross_block(): jnp.concatenate([real_part, imag_part], axis=-1)  171 us
    unnamed x3, waiting for transfers between devices  43.3 us
  transfers between devices with their start and end apart: 2, of which 2 were waited for; matrix products, arithmetic and copies ran while one was open for 0% of the time, Pallas kernels for 0%

commit v1 on v0

--- a/solution.py
+++ b/solution.py
@@ -8,6 +8,27 @@
 W = 2
 LAGS = 64
 FBLK = 128
+
+
+def gather_around(x, axis, dim):
+    count, index, extent = (lax.axis_size(axis), lax.axis_index(axis), x.shape[dim])
+    right = [(i, (i + 1) % count) for i in range(count)]
+    behind = [(i, (i - 1) % count) for i in range(count)]
+    out = jnp.zeros((*x.shape[:dim], count * extent, *x.shape[dim + 1 :]), x.dtype)
+    out = lax.dynamic_update_slice_in_dim(out, x, index * extent, axis=dim)
+    from_left = from_right = x
+    half = count // 2
+    for step in range(1, half + 1):
+        from_left = lax.ppermute(from_left, axis, right)
+        out = lax.dynamic_update_slice_in_dim(
+            out, from_left, (index - step) % count * extent, axis=dim
+        )
+        if step < count - half:
+            from_right = lax.ppermute(from_right, axis, behind)
+            out = lax.dynamic_update_slice_in_dim(
+                out, from_right, (index + step) % count * extent, axis=dim
+            )
+    return out
 
 
 def phase_table(freq_first, width):
@@ -67,7 +88,7 @@
     own_index = lax.axis_index("tiles")
     wanted = lax.dynamic_index_in_dim(requests, own_index, 0, keepdims=False)
     empty = jnp.zeros((wanted.shape[0],) + spectra.shape[1:], jnp.bfloat16)
-    shards = lax.all_gather(spectra, "tiles", axis=0, tiled=True)
+    shards = gather_around(spectra, "tiles", 0)
     inside = (wanted >= 0) & (wanted < shards.shape[0])
     taken = jnp.take(shards, jnp.clip(wanted, 0, shards.shape[0] - 1), axis=0)
     needed = jnp.where(inside[:, None, None, None, None], taken, empty)

time: 1020 us -> 1210 us (1.19)
  waiting for transfers between devices: 231 us -> 332 us
  local copies, waits for them, and re-layouts: 53.4 us -> 101 us
  starting transfers between devices: 0.04 us -> 32 us
    ppermute x0 -> x15, waiting for transfers between devices: none -> 286 us  [the longest x8 284 us: gather_around(): from_left = lax.ppermute(from_left, axis, right)]
    all_gather x1 -> x0, waiting for transfers between devices: 187 us -> none  [per_device(): shards = lax.all_gather(spectra, 'tiles', axis=0, tiled=True)]
    ppermute x0 -> x15, starting transfers between devices: none -> 32 us  [the longest x7 29.5 us: gather_around(): from_right = lax.ppermute(from_right, axis, behind)]
    dynamic_update_slice x0 -> x16, local copies, waits for them, and re-layouts: none -> 30.7 us  [the longest x8 15.3 us: gather_around(): lax.dynamic_update_slice_in_dim(out, from_left, (index - step) % count *...]
    unnamed x3 -> x2, waiting for transfers between devices: 43.3 us -> 45.3 us
  transfers between devices with their start and end apart: 2 -> 16, of which waited for: 2 -> 10; matrix products, arithmetic and copies ran while one was open for 0% -> 4% of each run, Pallas kernels for 0% -> 0%
where the time goes in v1:
time: 1210 us; the launch traced here: 1200 us
  other arithmetic  477 us (39%)
  waiting for transfers between devices  332 us (27%)
  matrix products  217 us (18%)
  local copies, waits for them, and re-layouts  101 us (8%)
  starting transfers between devices  32 us (3%)
  between operations  25.6 us (2%)
  loops' own time  17.3 us (1%)
    ppermute x8, waiting for transfers between devices, gather_around(): from_left = lax.ppermute(from_left, axis, right)  284 us
    reduce_sum x24, other arithmetic, cross_block(): jnp.sum(left_wide[:, 0, :, None, :] * right_wide[:, 0, None, :, :] + left...  280 us
    dot_general x24, matrix products, block_step(): lax.dot_general(phases, stacked, (((0,), (1,)), ((), ())), preferred_elem...  217 us
    concatenate x24, other arithmetic, cross_block(): jnp.concatenate([real_part, imag_part], axis=-1)  172 us
    unnamed x2, waiting for transfers between devices  45.3 us
    ppermute x7, starting transfers between devices, gather_around(): from_right = lax.ppermute(from_right, axis, behind)  29.5 us
  transfers between devices with their start and end apart: 16, of which 10 were waited for; matrix products, arithmetic and copies ran while one was open for 4% of the time, Pallas kernels for 0%

profile of v1, /device:TPU:1, one launch (start us, length us, event | category | flops | bytes accessed | tf_op | source)
XLA Modules:
  0.0 1202.2 jit_solution(11175479433987839671)
XLA Ops:
  13.6 45.6 %collective-permute-done = bf16[2,2,2,128,1024]{4,3,2,1,0:T(8,128)(2,1)S(1)} collective-permute-done((bf16[2,2,2,128,1024]{4,3,2,1,0:T(8,128)(2,1)}, bf16[2,2,2,128,1024]{4,3,2,1,0:T(8,128)(2,1)S(1)}, u32[]{:S(2)}, u32[]{:S(2)}) %collective-permute-start) | collective-permute-done | bytes 2097184 | tf_op jit(solution)/shard_map/ppermute | solution.py:22
  63.9 44.4 %collective-permute-done.2 = bf16[2,2,2,128,1024]{4,3,2,1,0:T(8,128)(2,1)S(1)} collective-permute-done((bf16[2,2,2,128,1024]{4,3,2,1,0:T(8,128)(2,1)S(1)}, bf16[2,2,2,128,1024]{4,3,2,1,0:T(8,128)(2,1)S(1)}, u32[]{:S(2)}, u32[]{:S(2)}) %collective-permute-start.2) | collective-permute-done | bytes 2097184 | tf_op jit(solution)/shard_map/ppermute | solution.py:22
  113.2 43.4 %collective-permute-done.4 = bf16[2,2,2,128,1024]{4,3,2,1,0:T(8,128)(2,1)S(1)} collective-permute-done((bf16[2,2,2,128,1024]{4,3,2,1,0:T(8,128)(2,1)S(1)}, bf16[2,2,2,128,1024]{4,3,2,1,0:T(8,128)(2,1)S(1)}, u32[]{:S(2)}, u32[]{:S(2)}) %collective-permute-start.4) | collective-permute-done | bytes 2097184 | tf_op jit(solution)/shard_map/ppermute | solution.py:22
  161.5 42.5 %collective-permute-done.6 = bf16[2,2,2,128,1024]{4,3,2,1,0:T(8,128)(2,1)S(1)} collective-permute-done((bf16[2,2,2,128,1024]{4,3,2,1,0:T(8,128)(2,1)S(1)}, bf16[2,2,2,128,1024]{4,3,2,1,0:T(8,128)(2,1)S(1)}, u32[]{:S(2)}, u32[]{:S(2)}) %collective-permute-start.6) | collective-permute-done | bytes 2097184 | tf_op jit(solution)/shard_map/ppermute | solution.py:22
  208.9 41.6 %collective-permute-done.8 = bf16[2,2,2,128,1024]{4,3,2,1,0:T(8,128)(2,1)S(1)} collective-permute-done((bf16[2,2,2,128,1024]{4,3,2,1,0:T(8,128)(2,1)S(1)}, bf16[2,2,2,128,1024]{4,3,2,1,0:T(8,128)(2,1)S(1)}, u32[]{:S(2)}, u32[]{:S(2)}) %collective-permute-start.8) | collective-permute-done | bytes 2097184 | tf_op jit(solution)/shard_map/ppermute | solution.py:22
  255.3 40.8 %collective-permute-done.10 = bf16[2,2,2,128,1024]{4,3,2,1,0:T(8,128)(2,1)} collective-permute-done((bf16[2,2,2,128,1024]{4,3,2,1,0:T(8,128)(2,1)S(1)}, bf16[2,2,2,128,1024]{4,3,2,1,0:T(8,128)(2,1)}, u32[]{:S(2)}, u32[]{:S(2)}) %collective-permute-start.10) | collective-permute-done | bytes 2097184 | tf_op jit(solution)/shard_map/ppermute | solution.py:22
  369.8 15.2 %collective-permute-done.14 = bf16[2,2,2,128,1024]{4,3,2,1,0:T(8,128)(2,1)S(1)} collective-permute-done((bf16[2,2,2,128,1024]{4,3,2,1,0:T(8,128)(2,1)}, bf16[2,2,2,128,1024]{4,3,2,1,0:T(8,128)(2,1)S(1)}, u32[]{:S(2)}, u32[]{:S(2)}) %collective-permute-start.14) | collective-permute-done | bytes 2097184 | tf_op jit(solution)/shard_map/ppermute | solution.py:22
  399.5 237.0 %while.40 = (s32[]{:T(128)}, f32[64,16384]{1,0:T(8,128)}, s32[8]{0:T(128)S(1)}, s32[]{:T(128)}, bf16[2,2,128,1024]{3,2,1,0:T(8,128)(2,1)S(1)}, /*index=5*/bf16[2...) while((s32[]{:T(128)}, f32[64,16384]{1,0:T(8,128)}, ...), condition=%wide.region_3.5_spmd.clone, body=%wide.region_0.4_spmd.clone.sunk | while | flops 585442176 | bytes 44893884 | solution.py:82
  401.1 11.7 add_reduce_fusion.6
  429.7 11.7 add_reduce_fusion.6
  459.4 11.7 add_reduce_fusion.6
  489.2 11.7 add_reduce_fusion.6
  519.0 11.7 add_reduce_fusion.6
  548.8 11.7 add_reduce_fusion.6
  578.5 11.7 add_reduce_fusion.6
  639.9 244.5 %while.41 = (s32[]{:T(128)}, f32[64,16384]{1,0:T(8,128)}, s32[8]{0:T(128)S(1)}, s32[]{:T(128)}, bf16[2,2,128,1024]{3,2,1,0:T(8,128)(2,1)}, /*index=5*/bf16[2,2,1...) while((s32[]{:T(128)}, f32[64,16384]{1,0:T(8,128)}, s32[8]{0:T(128)S(1)}, ...), condition=%wide.region_7.9_spmd.clone, body=%wide.region_4.8_spmd.clone.sunk | while | flops 585442176 | bytes 44893884 | solution.py:82
  642.4 11.7 add_reduce_fusion.7
  671.9 11.7 add_reduce_fusion.7
  702.6 11.7 add_reduce_fusion.7
  733.3 11.7 add_reduce_fusion.7
  764.0 11.7 add_reduce_fusion.7
  794.7 11.7 add_reduce_fusion.7
  825.4 11.7 add_reduce_fusion.7
  856.1 11.7 add_reduce_fusion.7
  889.0 243.9 %while.42 = (s32[]{:T(128)}, f32[64,16384]{1,0:T(8,128)}, s32[8]{0:T(128)S(1)}, s32[]{:T(128)}, bf16[2,2,128,1024]{3,2,1,0:T(8,128)(2,1)}, /*index=5*/bf16[2,2,1...) while((s32[]{:T(128)}, f32[64,16384]{1,0:T(8,128)}, s32[8]{0:T(128)S(1)}, ...), condition=%wide.region_11.13_spmd.clone, body=%wide.region_8.12_spmd.clone.sunk | while | flops 585442176 | bytes 44893884 | solution.py:82
  891.6 11.7 add_reduce_fusion.8
  951.6 11.7 add_reduce_fusion.8
  982.2 11.7 add_reduce_fusion.8
  1012.8 11.7 add_reduce_fusion.8
  1043.5 11.7 add_reduce_fusion.8
  1074.1 11.7 add_reduce_fusion.8
  1147.2 45.3 %reduce-scatter.5.cloned.1.call-done = bf16[8,49152]{1,0:T(8,128)(2,1)} async-done(((bf16[64,49152]{1,0:T(8,128)(2,1)}), bf16[8,49152]{1,0:T(8,128)(2,1)}) %reduce-scatter.5.cloned.1.call-update) | async-done | bytes 786448
  (371 shorter events, 595.3 us)
Async XLA Ops:
  6.5 1186.0 %reduce-scatter.5.cloned.1.call-start = ((), (), s32[]{:S(2)}) async-start(), calls=%async_computation.1 | async-start | bytes 7077888
  6.5 52.6 %collective-permute-start = (bf16[2,2,2,128,1024]{4,3,2,1,0:T(8,128)(2,1)}, bf16[2,2,2,128,1024]{4,3,2,1,0:T(8,128)(2,1)S(1)}, u32[]{:S(2)}, u32[]{:S(2)}) collective-permute-start(bf16[2,2,2,128,1024]{4,3,2,1,0:T(8,128)(2,1)} %param.12), channel_id=1, source_target_pairs={{0,8},{8,16},{16,24},{24,32},{32,40},{40,48},{48,56},{56,64},{64,7... | collective-permute-start | bytes 6291464 | tf_op jit(solution)/shard_map/ppermute | solution.py:22
  9.0 50.1 %collective-permute-start.1 = (bf16[2,2,2,128,1024]{4,3,2,1,0:T(8,128)(2,1)}, bf16[2,2,2,128,1024]{4,3,2,1,0:T(8,128)(2,1)S(1)}, u32[]{:S(2)}, u32[]{:S(2)}) collective-permute-start(bf16[2,2,2,128,1024]{4,3,2,1,0:T(8,128)(2,1)} %param.12), channel_id=1, source_target_pairs={{0,120},{8,0},{16,8},{24,16},{32,24},{40,32},{48,40},{56,48},{64,5... | collective-permute-start | bytes 6291464 | tf_op jit(solution)/shard_map/ppermute | solution.py:27
  59.1 97.5 %copy-start.6 = (bf16[2,2,2,128,1024]{4,3,2,1,0:T(8,128)(2,1)}, bf16[2,2,2,128,1024]{4,3,2,1,0:T(8,128)(2,1)S(1)}, u32[]{:S(2)}) copy-start(bf16[2,2,2,128,1024]{4,3,2,1,0:T(8,128)(2,1)S(1)} %collective-permute-done) | copy-start | bytes 6291460
  59.1 49.2 %collective-permute-start.2 = (bf16[2,2,2,128,1024]{4,3,2,1,0:T(8,128)(2,1)S(1)}, bf16[2,2,2,128,1024]{4,3,2,1,0:T(8,128)(2,1)S(1)}, u32[]{:S(2)}, u32[]{:S(2)}) collective-permute-start(bf16[2,2,2,128,1024]{4,3,2,1,0:T(8,128)(2,1)S(1)} %collective-permute-done), channel_id=1, source_target_pairs={{0,8},{8,16},{16,24},{24,32},{32,40},{40,48},{48,56},{56,64},{64,7... | collective-permute-start | bytes 6291464 | tf_op jit(solution)/shard_map/ppermute | solution.py:22
  59.1 49.2 %collective-permute-start.3 = (bf16[2,2,2,128,1024]{4,3,2,1,0:T(8,128)(2,1)S(1)}, bf16[2,2,2,128,1024]{4,3,2,1,0:T(8,128)(2,1)S(1)}, u32[]{:S(2)}, u32[]{:S(2)}) collective-permute-start(bf16[2,2,2,128,1024]{4,3,2,1,0:T(8,128)(2,1)S(1)} %collective-permute-done.1), channel_id=1, source_target_pairs={{0,120},{8,0},{16,8},{24,16},{32,24},{40,32},{48,40},{56,48},{64,5... | collective-permute-start | bytes 6291464 | tf_op jit(solution)/shard_map/ppermute | solution.py:27
  108.4 48.3 %collective-permute-start.4 = (bf16[2,2,2,128,1024]{4,3,2,1,0:T(8,128)(2,1)S(1)}, bf16[2,2,2,128,1024]{4,3,2,1,0:T(8,128)(2,1)S(1)}, u32[]{:S(2)}, u32[]{:S(2)}) collective-permute-start(bf16[2,2,2,128,1024]{4,3,2,1,0:T(8,128)(2,1)S(1)} %collective-permute-done.2), channel_id=1, source_target_pairs={{0,8},{8,16},{16,24},{24,32},{32,40},{40,48},{48,56},{56,64},{64,7... | collective-permute-start | bytes 6291464 | tf_op jit(solution)/shard_map/ppermute | solution.py:22
  109.7 46.9 %copy-start.4 = (bf16[2,2,2,128,1024]{4,3,2,1,0:T(8,128)(2,1)}, bf16[2,2,2,128,1024]{4,3,2,1,0:T(8,128)(2,1)S(1)}, u32[]{:S(2)}) copy-start(bf16[2,2,2,128,1024]{4,3,2,1,0:T(8,128)(2,1)S(1)} %collective-permute-done.3) | copy-start | bytes 6291460
  109.7 46.9 %collective-permute-start.5 = (bf16[2,2,2,128,1024]{4,3,2,1,0:T(8,128)(2,1)S(1)}, bf16[2,2,2,128,1024]{4,3,2,1,0:T(8,128)(2,1)S(1)}, u32[]{:S(2)}, u32[]{:S(2)}) collective-permute-start(bf16[2,2,2,128,1024]{4,3,2,1,0:T(8,128)(2,1)S(1)} %collective-permute-done.3), channel_id=1, source_target_pairs={{0,120},{8,0},{16,8},{24,16},{32,24},{40,32},{48,40},{56,48},{64,5... | collective-permute-start | bytes 6291464 | tf_op jit(solution)/shard_map/ppermute | solution.py:27
  156.7 4.9 copy-start.8
  156.7 47.4 %collective-permute-start.6 = (bf16[2,2,2,128,1024]{4,3,2,1,0:T(8,128)(2,1)S(1)}, bf16[2,2,2,128,1024]{4,3,2,1,0:T(8,128)(2,1)S(1)}, u32[]{:S(2)}, u32[]{:S(2)}) collective-permute-start(bf16[2,2,2,128,1024]{4,3,2,1,0:T(8,128)(2,1)S(1)} %collective-permute-done.4), channel_id=1, source_target_pairs={{0,8},{8,16},{16,24},{24,32},{32,40},{40,48},{48,56},{56,64},{64,7... | collective-permute-start | bytes 6291464 | tf_op jit(solution)/shard_map/ppermute | solution.py:22
  156.7 47.3 %copy-start.10 = (bf16[2,2,2,128,1024]{4,3,2,1,0:T(8,128)(2,1)}, bf16[2,2,2,128,1024]{4,3,2,1,0:T(8,128)(2,1)S(1)}, u32[]{:S(2)}) copy-start(bf16[2,2,2,128,1024]{4,3,2,1,0:T(8,128)(2,1)S(1)} %collective-permute-done.5) | copy-start | bytes 6291460
  156.7 47.3 %collective-permute-start.7 = (bf16[2,2,2,128,1024]{4,3,2,1,0:T(8,128)(2,1)S(1)}, bf16[2,2,2,128,1024]{4,3,2,1,0:T(8,128)(2,1)S(1)}, u32[]{:S(2)}, u32[]{:S(2)}) collective-permute-start(bf16[2,2,2,128,1024]{4,3,2,1,0:T(8,128)(2,1)S(1)} %collective-permute-done.5), channel_id=1, source_target_pairs={{0,120},{8,0},{16,8},{24,16},{32,24},{40,32},{48,40},{56,48},{64,5... | collective-permute-start | bytes 6291464 | tf_op jit(solution)/shard_map/ppermute | solution.py:27
  204.0 1.4 copy-start.12
  204.0 46.5 %collective-permute-start.8 = (bf16[2,2,2,128,1024]{4,3,2,1,0:T(8,128)(2,1)S(1)}, bf16[2,2,2,128,1024]{4,3,2,1,0:T(8,128)(2,1)S(1)}, u32[]{:S(2)}, u32[]{:S(2)}) collective-permute-start(bf16[2,2,2,128,1024]{4,3,2,1,0:T(8,128)(2,1)S(1)} %collective-permute-done.6), channel_id=1, source_target_pairs={{0,8},{8,16},{16,24},{24,32},{32,40},{40,48},{48,56},{56,64},{64,7... | collective-permute-start | bytes 6291464 | tf_op jit(solution)/shard_map/ppermute | solution.py:22
  205.4 45.1 %copy-start.14 = (bf16[2,2,2,128,1024]{4,3,2,1,0:T(8,128)(2,1)}, bf16[2,2,2,128,1024]{4,3,2,1,0:T(8,128)(2,1)S(1)}, u32[]{:S(2)}) copy-start(bf16[2,2,2,128,1024]{4,3,2,1,0:T(8,128)(2,1)S(1)} %collective-permute-done.7) | copy-start | bytes 6291460
  205.4 45.1 %collective-permute-start.9 = (bf16[2,2,2,128,1024]{4,3,2,1,0:T(8,128)(2,1)S(1)}, bf16[2,2,2,128,1024]{4,3,2,1,0:T(8,128)(2,1)}, u32[]{:S(2)}, u32[]{:S(2)}) collective-permute-start(bf16[2,2,2,128,1024]{4,3,2,1,0:T(8,128)(2,1)S(1)} %collective-permute-done.7), channel_id=1, source_target_pairs={{0,120},{8,0},{16,8},{24,16},{32,24},{40,32},{48,40},{56,48},{64,5... | collective-permute-start | bytes 6291464 | tf_op jit(solution)/shard_map/ppermute | solution.py:27
  250.5 45.6 %collective-permute-start.10 = (bf16[2,2,2,128,1024]{4,3,2,1,0:T(8,128)(2,1)S(1)}, bf16[2,2,2,128,1024]{4,3,2,1,0:T(8,128)(2,1)}, u32[]{:S(2)}, u32[]{:S(2)}) collective-permute-start(bf16[2,2,2,128,1024]{4,3,2,1,0:T(8,128)(2,1)S(1)} %collective-permute-done.8), channel_id=1, source_target_pairs={{0,8},{8,16},{16,24},{24,32},{32,40},{40,48},{48,56},{56,64},{64,7... | collective-permute-start | bytes 6291464 | tf_op jit(solution)/shard_map/ppermute | solution.py:22
  251.8 72.6 %collective-permute-start.11 = (bf16[2,2,2,128,1024]{4,3,2,1,0:T(8,128)(2,1)}, bf16[2,2,2,128,1024]{4,3,2,1,0:T(8,128)(2,1)}, u32[]{:S(2)}, u32[]{:S(2)}) collective-permute-start(bf16[2,2,2,128,1024]{4,3,2,1,0:T(8,128)(2,1)} %collective-permute-done.9), channel_id=1, source_target_pairs={{0,120},{8,0},{16,8},{24,16},{32,24},{40,32},{48,40},{56,48},{64,5... | collective-permute-start | bytes 6291464 | tf_op jit(solution)/shard_map/ppermute | solution.py:27
  296.1 44.9 %collective-permute-start.12 = (bf16[2,2,2,128,1024]{4,3,2,1,0:T(8,128)(2,1)}, bf16[2,2,2,128,1024]{4,3,2,1,0:T(8,128)(2,1)}, u32[]{:S(2)}, u32[]{:S(2)}) collective-permute-start(bf16[2,2,2,128,1024]{4,3,2,1,0:T(8,128)(2,1)} %collective-permute-done.10), channel_id=1, source_target_pairs={{0,8},{8,16},{16,24},{24,32},{32,40},{40,48},{48,56},{56,64},{64,7... | collective-permute-start | bytes 6291464 | tf_op jit(solution)/shard_map/ppermute | solution.py:22
  311.1 11.7 copy-start.1
  311.2 18.0 %copy-start.7 = (bf16[2,2,2,128,1024]{4,3,2,1,0:T(8,128)(2,1)S(1)}, bf16[2,2,2,128,1024]{4,3,2,1,0:T(8,128)(2,1)}, u32[]{:S(2)}) copy-start(bf16[2,2,2,128,1024]{4,3,2,1,0:T(8,128)(2,1)} %copy-done.6) | copy-start | bytes 6291460
  322.8 19.8 %copy-start.3 = (bf16[2,2,2,128,1024]{4,3,2,1,0:T(8,128)(2,1)S(1)}, bf16[2,2,2,128,1024]{4,3,2,1,0:T(8,128)(2,1)}, u32[]{:S(2)}) copy-start(bf16[2,2,2,128,1024]{4,3,2,1,0:T(8,128)(2,1)} %copy-done.2) | copy-start | bytes 6291460
  324.4 19.8 %copy-start.5 = (bf16[2,2,2,128,1024]{4,3,2,1,0:T(8,128)(2,1)S(1)}, bf16[2,2,2,128,1024]{4,3,2,1,0:T(8,128)(2,1)}, u32[]{:S(2)}) copy-start(bf16[2,2,2,128,1024]{4,3,2,1,0:T(8,128)(2,1)} %copy-done.4) | copy-start | bytes 6291460
  324.4 44.0 %collective-permute-start.13 = (bf16[2,2,2,128,1024]{4,3,2,1,0:T(8,128)(2,1)}, bf16[2,2,2,128,1024]{4,3,2,1,0:T(8,128)(2,1)S(1)}, u32[]{:S(2)}, u32[]{:S(2)}) collective-permute-start(bf16[2,2,2,128,1024]{4,3,2,1,0:T(8,128)(2,1)} %collective-permute-done.11), channel_id=1, source_target_pairs={{0,120},{8,0},{16,8},{24,16},{32,24},{40,32},{48,40},{56,48},{64,5... | collective-permute-start | bytes 6291464 | tf_op jit(solution)/shard_map/ppermute | solution.py:27
  330.7 15.0 %copy-start.9 = (bf16[2,2,2,128,1024]{4,3,2,1,0:T(8,128)(2,1)S(1)}, bf16[2,2,2,128,1024]{4,3,2,1,0:T(8,128)(2,1)}, u32[]{:S(2)}) copy-start(bf16[2,2,2,128,1024]{4,3,2,1,0:T(8,128)(2,1)} %copy-done.8) | copy-start | bytes 6291460
  341.0 43.9 %collective-permute-start.14 = (bf16[2,2,2,128,1024]{4,3,2,1,0:T(8,128)(2,1)}, bf16[2,2,2,128,1024]{4,3,2,1,0:T(8,128)(2,1)S(1)}, u32[]{:S(2)}, u32[]{:S(2)}) collective-permute-start(bf16[2,2,2,128,1024]{4,3,2,1,0:T(8,128)(2,1)} %collective-permute-done.12), channel_id=1, source_target_pairs={{0,8},{8,16},{16,24},{24,32},{32,40},{40,48},{48,56},{56,64},{64,7... | collective-permute-start | bytes 6291464 | tf_op jit(solution)/shard_map/ppermute | solution.py:22
  342.6 4.5 copy-start.11
  344.1 4.6 copy-start.13
  345.7 4.6 copy-start.15
  347.2 4.7 copy-start.17
  1133.0 3.5 copy-start
  (2 other events, 2.7 us)
Sparse Core Ops, SparseCore 0:
  1147.3 45.1 reduce-scatter.4
